TPU v7x, 256 devices: a whole 4x4x8 slice. The times are simulated.
256 devices in a mesh: tok: 32 (over z, y_hi, core), row: 2 (over y_lo), col: 4 (over x).
Axes of the slice: x: 4, y: 4 (y_hi: 2, y_lo: 2; y = y_hi * 2 + y_lo), z: 8, core: 2. Of those that a mesh axis runs over, the one named last changes fastest.
Arguments:
- activations: bfloat16 [11264, 4096], P(('tok', 'row'), 'col'), may hold values from -512 to 512
- norm_gain: bfloat16 [4096], P('col'), may hold values from 1.5 to 10
- qkv_weight: bfloat16 [4096, 16, 384], P('row', 'col'), may hold values from -0.09375 to 0.09375
- doc_ids: int32 [11264], P(('tok', 'row')), may hold values from 0 to 3, never falling along the last dimension, each value on 1 to 8448 neighbouring positions
Outputs:
- attended: bfloat16 [11264, 2048], P(('tok', 'row'), 'col')
Inputs may be any that keep to these rules, and one draw needn't show every extreme that they name: `doc_ids`: never falls along the sequence; each of the 4 documents holds 1 to 8448 tokens and one holds exactly 8448.
All inputs are finite; a program needn't handle non-finite values.
Results may differ from a plain program's by a relative error of at most 0.007.
The roundings to bfloat16 on the way count: a program that leaves them out, or rounds other values in their place, can miss the bound.
Values may be sent and summed in bfloat16 or wider, within the bound.
A program may use at most 128 MiB of HBM per device.

v0:
```python
import math
import jax
import jax.numpy as jnp
from jax import lax
from jax.sharding import PartitionSpec as P


def rotate(vectors, places):
    half = vectors.shape[-1] // 2
    spacing = jnp.arange(half).astype(jnp.float32) * (2.0 / vectors.shape[-1])
    inverse = jnp.power(10000.0, -spacing)
    angles = places.astype(jnp.float32)[:, None] * inverse[None, :]
    cosine = jnp.cos(angles)[:, None, :]
    sine = jnp.sin(angles)[:, None, :]
    first_half = vectors[..., :half]
    second_half = vectors[..., half:]
    return jnp.concatenate(
        [first_half * cosine - second_half * sine, first_half * sine + second_half * cosine],
        axis=-1,
    )


def per_device(activations, norm_gain, qkv_weight, doc_ids):
    row_count = activations.shape[0]
    whole, gain_whole = (
        lax.all_gather(activations, "col", axis=1, tiled=True),
        lax.all_gather(norm_gain, "col", axis=0, tiled=True),
    )
    widened = whole.astype(jnp.float32)
    mean_square = jnp.mean(widened * widened, axis=1, keepdims=True)
    normed = (widened * lax.rsqrt(mean_square + 1e-05) * gain_whole.astype(jnp.float32)).astype(
        jnp.bfloat16
    )
    span, local_heads, width = qkv_weight.shape
    head_size = width // 3
    flat_weight = qkv_weight.reshape(span, local_heads * width)
    projected = jnp.dot(
        normed,
        lax.all_gather(flat_weight, "row", axis=0, tiled=True),
        preferred_element_type=jnp.float32,
    )
    projected = projected.reshape(row_count, local_heads, width)
    first = (lax.axis_index("tok") * lax.axis_size("row") + lax.axis_index("row")) * row_count
    places = first + jnp.arange(row_count, dtype=jnp.int32)
    query = rotate(projected[..., :head_size], places).astype(jnp.bfloat16)
    keys = rotate(projected[..., head_size : 2 * head_size], places).astype(jnp.bfloat16)
    values = projected[..., 2 * head_size :].astype(jnp.bfloat16)
    scale = 1.0 / math.sqrt(head_size)

    def update(state, block_keys, block_values, block_docs, key_places):
        running, totals, summed = state
        scores = (
            jnp.einsum("qhd,khd->hqk", query, block_keys, preferred_element_type=jnp.float32)
            * scale
        )
        visible = (key_places[None, None, :] <= places[None, :, None]) & (
            block_docs[None, None, :] == doc_ids[None, :, None]
        )
        masked = jnp.where(visible, scores, -jnp.inf)
        newest = jnp.maximum(running, jnp.max(masked, axis=2))
        factor = jnp.exp(running - newest)
        exponentials = jnp.where(visible, jnp.exp(masked - newest[:, :, None]), 0.0)
        weights = exponentials.astype(jnp.bfloat16)
        totals = totals * factor + jnp.sum(exponentials, axis=2)
        summed = summed * factor.T[:, :, None] + jnp.einsum(
            "hqk,khd->qhd", weights, block_values, preferred_element_type=jnp.float32
        )
        return (newest, totals, summed)

    initial = (
        jnp.full((local_heads, row_count), -1e30, jnp.float32),
        jnp.zeros((local_heads, row_count), jnp.float32),
        jnp.zeros((row_count, local_heads, head_size), jnp.float32),
    )
    pair_keys, pair_values, pair_docs = (
        lax.all_gather(keys, "row", axis=0, tiled=True),
        lax.all_gather(values, "row", axis=0, tiled=True),
        lax.all_gather(doc_ids, "row", axis=0, tiled=True),
    )
    state = initial
    block_keys = lax.all_gather(pair_keys, "tok", axis=0, tiled=True)
    block_values = lax.all_gather(pair_values, "tok", axis=0, tiled=True)
    block_docs = lax.all_gather(pair_docs, "tok", axis=0, tiled=True)
    count = block_keys.shape[0]
    key_places = jnp.arange(count, dtype=jnp.int32)
    rounds = count // 1024
    stacked = (
        block_keys.reshape(rounds, 1024, local_heads, head_size),
        block_values.reshape(rounds, 1024, local_heads, head_size),
        block_docs.reshape(rounds, 1024),
        key_places.reshape(rounds, 1024),
    )

    def advance(carried, blocks):
        return (update(carried, blocks[0], blocks[1], blocks[2], blocks[3]), None)

    state, unused = lax.scan(advance, state, stacked)
    running, totals, summed = state
    attended = summed / totals.T[:, :, None]
    return attended.reshape(row_count, local_heads * head_size).astype(jnp.bfloat16)


def solution(mesh):
    placed = (P(("tok", "row"), "col"), P("col"), P("row", "col", None), P(("tok", "row")))
    return jax.shard_map(
        per_device, mesh=mesh, in_specs=placed, out_specs=P(("tok", "row"), "col"), check_vma=False
    )
```

profile of v0, /device:TPU:1, one launch (start us, length us, event | category | flops | bytes accessed | tf_op | source)
XLA Modules:
  0.0 528.5 jit_solution(10905290454342149251)
XLA Ops:
  7.3 6.6 %copy.35 = bf16[256,8,4,384]{3,1,2,0:T(8,128)(2,1)} copy(bf16[256,8,4,384]{3,2,1,0:T(4,128)(2,1)} %bitcast.72) | data formatting | bytes 12582912
  14.5 9.3 %all_gather.30 = bf16[4096]{0:T(1024)(128)(2,1)S(1)} all-gather(bf16[1024]{0:T(1024)(128)(2,1)S(1)} %copy-done.1), channel_id=1, replica_groups=mesh['tok'=32,'row'=2,'col'=4] {'col'}, dimensions={0}, use_global_device_ids=true | all-gather | bytes 10240 | tf_op jit(solution)/shard_map/all_gather | solution.py:27
  24.3 16.4 %all-gather.5.cloned.1.call-done = bf16[176,4096]{1,0:T(8,128)(2,1)} async-done(((bf16[176,1024]{1,0:T(8,128)(2,1)}), bf16[176,4096]{1,0:T(8,128)(2,1)}) %all-gather.5.cloned.1.call-update) | async-done | bytes 1441808 | tf_op jit(solution)/shard_map/all_gather | solution.py:26
  40.7 1.7 fusion.26
  42.4 158.1 %all-gather.7.cloned.1.call-done = bf16[4096,1536]{1,0:T(8,128)(2,1)} async-done(((bf16[2048,1536]{1,0:T(8,128)(2,1)}), bf16[4096,1536]{1,0:T(8,128)(2,1)}) %all-gather.7.cloned.1.call-update) | async-done | bytes 12582928 | tf_op jit(solution)/shard_map/all_gather | solution.py:39
  200.5 7.5 %fusion.29 = f32[176,1536]{1,0:T(8,128)S(1)} fusion(bf16[4096,1536]{1,0:T(8,128)(2,1)} %all-gather.7.cloned.1.call-done, bf16[176,4096]{1,0:T(8,128)(2,1)} %all-gather.5.cloned.1.call-done, f32[4096]{0:T(1024)S(1)} %convert_element_type.38, f32[176]{0:T(256)S(1)} %add_rsqrt_fusion), kind=kOutput, calls=%fused_computation.35 | convolution fusion | flops 2217476096 | bytes 15123136 | tf_op jit(solution)/shard_map/dot_general | solution.py:37
  209.3 6.0 %all_gather.32 = bf16[352,4,128]{2,0,1:T(8,128)(2,1)} all-gather(bf16[176,4,128]{2,0,1:T(8,128)(2,1)S(1)} %pad_maximum_fusion), channel_id=1, replica_groups=mesh['tok'=32,'row'=2,'col'=4] {'row'}, dimensions={0}, use_global_device_ids=true | all-gather | bytes 540672 | tf_op jit(solution)/shard_map/all_gather | solution.py:76
  215.5 5.1 all_gather.34
  223.3 3.1 all-reduce
  226.7 129.4 %all-reduce.1 = s32[11264]{0:T(1024)S(1)} all-reduce(s32[11264]{0:T(1024)S(1)} %dynamic-update-slice.1), channel_id=1, replica_groups=mesh['tok'=32,'row'=2,'col'=4] {'tok'}, use_global_device_ids=true, to_apply=%add.1 | all-reduce | flops 11264 | bytes 90112
  356.9 86.2 %all-gather.11.cloned.1.call-done = bf16[11264,4,128]{2,0,1:T(8,128)(2,1)} async-done(((bf16[352,4,128]{2,0,1:T(8,128)(2,1)}), bf16[11264,4,128]{2,0,1:T(8,128)(2,1)}) %all-gather.11.cloned.1.call-update) | async-done | bytes 11534352 | tf_op jit(solution)/shard_map/all_gather | solution.py:82
  443.1 77.1 %while.15 = (s32[]{:T(128)}, f32[4,176]{1,0:T(4,128)S(1)}, f32[4,176]{1,0:T(4,128)S(1)}, f32[176,4,128]{2,0,1:T(8,128)}, s32[11,1024]{1,0:T(8,128)}, /*index=5*/...) while((s32[]{:T(128)}, f32[4,176]{1,0:T(4,128)S(1)}, ...), condition=%wide.region_4.5_spmd.clone, body=%wide.region_1.4_spmd.clone.sunk | while | flops 379285824 | bytes 12442833 | solution.py:97
  444.1 2.0 fusion.49
  446.1 2.9 fusion.53
  449.0 1.0 fusion.51
  450.0 0.8 constant_dynamic-slice_fusion.3
  451.0 2.0 fusion.49
  453.0 3.0 fusion.53
  456.0 1.0 fusion.51
  458.0 2.0 fusion.49
  460.0 3.0 fusion.53
  463.0 1.0 fusion.51
  464.1 0.8 constant_dynamic-slice_fusion.3
  465.1 2.0 fusion.49
  467.0 3.0 fusion.53
  470.1 1.0 fusion.51
  472.1 2.0 fusion.49
  474.1 3.0 fusion.53
  477.1 1.0 fusion.51
  479.1 2.0 fusion.49
  481.1 3.0 fusion.53
  484.1 1.0 fusion.51
  486.1 2.0 fusion.49
  488.1 3.0 fusion.53
  491.1 1.0 fusion.51
  493.1 2.0 fusion.49
  495.1 3.0 fusion.53
  498.1 1.0 fusion.51
  500.1 2.0 fusion.49
  502.1 3.0 fusion.53
  505.1 1.0 fusion.51
  507.1 2.0 fusion.49
  509.1 3.0 fusion.53
  512.1 1.0 fusion.51
  514.2 2.0 fusion.49
  516.1 3.0 fusion.53
  519.2 1.0 fusion.51
  520.2 1.8 copy_bitcast_fusion
  (104 shorter events, 15.3 us)
Async XLA Ops:
  6.5 34.2 %all-gather.5.cloned.1.call-start = ((), (), s32[]{:S(2)}) async-start(), calls=%async_computation | async-start | bytes 1802240 | tf_op jit(solution)/shard_map/all_gather | solution.py:26
  7.3 193.3 %all-gather.7.cloned.1.call-start = ((), (), s32[]{:S(2)}) async-start(), calls=%async_computation.1 | async-start | bytes 18874368 | tf_op jit(solution)/shard_map/all_gather | solution.py:39
  13.9 0.7 copy-start.1
  13.9 343.0 %all-gather.9.cloned.1.call-start = ((), (), s32[]{:S(2)}) async-start(), calls=%async_computation.2 | async-start | bytes 11894784 | tf_op jit(solution)/shard_map/all_gather | solution.py:81
  208.9 11.8 %copy-start.3 = (u32[256]{0:T(256)S(1)}, u32[256]{0:T(256)}, u32[]{:S(2)}) copy-start(u32[256]{0:T(256)} %constant.56) | copy-start | bytes 3076
  208.9 12.4 %copy-start.2 = (u32[256]{0:T(256)S(1)}, u32[256]{0:T(256)}, u32[]{:S(2)}) copy-start(u32[256]{0:T(256)} %constant.61) | copy-start | bytes 3076
  208.9 14.1 %copy-start = (s32[176]{0:T(256)S(1)}, s32[176]{0:T(256)}, u32[]{:S(2)}) copy-start(s32[176]{0:T(256)} %param.9) | copy-start | bytes 2116
  215.3 227.8 %all-gather.11.cloned.1.call-start = ((), (), s32[]{:S(2)}) async-start(), calls=%async_computation.3 | async-start | bytes 11894784 | tf_op jit(solution)/shard_map/all_gather | solution.py:82
Sparse Core Ops, SparseCore 0:
  9.1 31.5 all-gather.4
  42.5 157.9 all-gather.6
  215.4 115.8 all-gather.8
  334.0 109.0 all-gather.10
where the time goes:
time: 530 us; the launch traced here: 529 us
  waiting for transfers between devices  262 us (49%)
  blocking collectives  153 us (29%)
  matrix products  62.1 us (12%)
  other arithmetic  18.5 us (3%)
  local copies, waits for them, and re-layouts  18.3 us (3%)
  between operations  14.5 us (3%)
    all_gather x1, waiting for transfers between devices, per_device(): lax.all_gather(flat_weight, 'row', axis=0, tiled=True)  158 us
    unnamed x2, blocking collectives  132 us
    all_gather x1, waiting for transfers between devices, per_device(): block_values = lax.all_gather(pair_values, 'tok', axis=0, tiled=True)  86.2 us
    dot_general x11, matrix products, update(): jnp.einsum('hqk,khd->qhd', weights, block_values, preferred_element_type=...  33 us
    dot_general x11, matrix products, update(): jnp.einsum('qhd,khd->hqk', query, block_keys, preferred_element_type=jnp....  21.6 us
    all_gather x1, waiting for transfers between devices, per_device(): lax.all_gather(activations, 'col', axis=1, tiled=True)  16.4 us
    reduce_sum x11, other arithmetic, update(): totals = totals * factor + jnp.sum(exponentials, axis=2)  10.7 us
  transfers between devices with their start and end apart: 4, of which 3 were waited for; matrix products, arithmetic and copies ran while one was open for 2% of the time, Pallas kernels for 0%

commit v1 on v0

--- a/solution.py
+++ b/solution.py
@@ -23,7 +23,9 @@
 def per_device(activations, norm_gain, qkv_weight, doc_ids):
     row_count = activations.shape[0]
     whole, gain_whole = (
-        lax.all_gather(activations, "col", axis=1, tiled=True),
+        jnp.concatenate(
+            lax.all_to_all(jnp.stack([activations] * lax.axis_size("col")), "col", 0, 0), axis=1
+        ),
         lax.all_gather(norm_gain, "col", axis=0, tiled=True),
     )
     widened = whole.astype(jnp.float32)

time: 530 us -> 508 us (0.958)
  waiting for transfers between devices: 262 us -> 217 us
  blocking collectives: 153 us -> 164 us
  local copies, waits for them, and re-layouts: 18.3 us -> 25.4 us
    all_gather x1, waiting for transfers between devices: 158 us -> 131 us  [per_device(): lax.all_gather(flat_weight, 'row', axis=0, tiled=True)]
    all_gather x1 -> x0, waiting for transfers between devices: 16.4 us -> none  [per_device(): lax.all_gather(activations, 'col', axis=1, tiled=True)]
    all_gather x1, blocking collectives: 9.3 us -> 20.1 us  [per_device(): lax.all_gather(norm_gain, 'col', axis=0, tiled=True)]
    reshape x1, local copies, waits for them, and re-layouts: 0.37 us -> 10.6 us  [per_device(): flat_weight = qkv_weight.reshape(span, local_heads * width)]
    unnamed x16, local copies, waits for them, and re-layouts: 8.87 us -> 2.76 us
  transfers between devices with their start and end apart: 4 -> 4, of which waited for: 3 -> 2; matrix products, arithmetic and copies ran while one was open for 2% -> 1% of each run, Pallas kernels for 0% -> 0%
where the time goes in v1:
time: 508 us; the launch traced here: 506 us
  waiting for transfers between devices  217 us (43%)
  blocking collectives  164 us (32%)
  matrix products  61.8 us (12%)
  local copies, waits for them, and re-layouts  25.4 us (5%)
  other arithmetic  17.8 us (4%)
  between operations  14.6 us (3%)
    unnamed x2, blocking collectives  133 us
    all_gather x1, waiting for transfers between devices, per_device(): lax.all_gather(flat_weight, 'row', axis=0, tiled=True)  131 us
    all_gather x1, waiting for transfers between devices, per_device(): block_values = lax.all_gather(pair_values, 'tok', axis=0, tiled=True)  86.2 us
    dot_general x11, matrix products, update(): jnp.einsum('hqk,khd->qhd', weights, block_values, preferred_element_type=...  32.9 us
    dot_general x11, matrix products, update(): jnp.einsum('qhd,khd->hqk', query, block_keys, preferred_element_type=jnp....  21.6 us
    all_gather x1, blocking collectives, per_device(): lax.all_gather(norm_gain, 'col', axis=0, tiled=True)  20.1 us
    reduce_sum x11, other arithmetic, update(): totals = totals * factor + jnp.sum(exponentials, axis=2)  10.7 us
    reshape x1, local copies, waits for them, and re-layouts, per_device(): flat_weight = qkv_weight.reshape(span, local_heads * width)  10.6 us
  transfers between devices with their start and end apart: 4, of which 2 were waited for; matrix products, arithmetic and copies ran while one was open for 1% of the time, Pallas kernels for 0%

profile of v1, /device:TPU:1, one launch (start us, length us, event | category | flops | bytes accessed | tf_op | source)
XLA Modules:
  0.0 505.6 jit_solution(15897941157685381817)
XLA Ops:
  6.5 10.6 %copy.18 = bf16[2048,4,384]{0,2,1:T(8,128)(2,1)} copy(bf16[2048,4,384]{2,1,0:T(4,128)(2,1)} %param.8) | data formatting | bytes 12582912 | tf_op jit(solution)/shard_map/reshape | solution.py:38
  18.2 1.3 stack.2
  19.5 4.8 all-to-all-start
  24.3 20.1 %all_gather.26 = bf16[4096]{0:T(1024)(128)(2,1)S(1)} all-gather(bf16[1024]{0:T(1024)(128)(2,1)S(1)} %copy-done.2), channel_id=1, replica_groups=mesh['tok'=32,'row'=2,'col'=4] {'col'}, dimensions={0}, use_global_device_ids=true | all-gather | bytes 10240 | tf_op jit(solution)/shard_map/all_gather | solution.py:29
  45.8 1.1 copy.13
  46.9 1.1 reshape.200
  48.0 130.6 %all-gather.4.cloned.1.call-done = bf16[4096,1536]{0,1:T(8,128)(2,1)} async-done(((bf16[2048,1536]{0,1:T(8,128)(2,1)}), bf16[4096,1536]{0,1:T(8,128)(2,1)}) %all-gather.4.cloned.1.call-update) | async-done | bytes 12582928 | tf_op jit(solution)/shard_map/all_gather | solution.py:41
  178.6 7.3 %fusion.31 = f32[176,4,384]{2,0,1:T(8,128)S(1)} fusion(bf16[176,4096,1]{1,0,2:T(8,128)(2,1)S(1)} %reshape.200, bf16[4,384,4096]{2,1,0:T(8,128)(2,1)} %bitcast.79), kind=kOutput, calls=%fused_computation.52 | convolution fusion | flops 2214592512 | bytes 15106048 | tf_op jit(solution)/shard_map/dot_general | solution.py:39
  186.4 6.0 %all_gather.28 = bf16[352,4,128]{2,0,1:T(8,128)(2,1)} all-gather(bf16[176,4,128]{2,0,1:T(8,128)(2,1)S(1)} %pad_maximum_fusion), channel_id=1, replica_groups=mesh['tok'=32,'row'=2,'col'=4] {'row'}, dimensions={0}, use_global_device_ids=true | all-gather | bytes 540672 | tf_op jit(solution)/shard_map/all_gather | solution.py:78
  192.5 5.1 %all_gather.30 = bf16[352,4,128]{2,0,1:T(8,128)(2,1)} all-gather(bf16[176,4,128]{2,0,1:T(8,128)(2,1)S(1)} %slice.41), channel_id=1, replica_groups=mesh['tok'=32,'row'=2,'col'=4] {'row'}, dimensions={0}, use_global_device_ids=true | all-gather | bytes 540672 | tf_op jit(solution)/shard_map/all_gather | solution.py:79
  200.6 3.1 all-reduce
  204.0 129.4 %all-reduce.1 = s32[11264]{0:T(1024)S(1)} all-reduce(s32[11264]{0:T(1024)S(1)} %dynamic-update-slice.1), channel_id=1, replica_groups=mesh['tok'=32,'row'=2,'col'=4] {'tok'}, use_global_device_ids=true, to_apply=%add.1 | all-reduce | flops 11264 | bytes 90112
  334.2 86.2 %all-gather.8.cloned.1.call-done = bf16[11264,4,128]{2,0,1:T(8,128)(2,1)} async-done(((bf16[352,4,128]{2,0,1:T(8,128)(2,1)}), bf16[11264,4,128]{2,0,1:T(8,128)(2,1)}) %all-gather.8.cloned.1.call-update) | async-done | bytes 11534352 | tf_op jit(solution)/shard_map/all_gather | solution.py:84
  420.3 76.9 %while.15 = (s32[]{:T(128)}, f32[4,176]{1,0:T(4,128)S(1)}, f32[4,176]{1,0:T(4,128)S(1)}, f32[176,4,128]{2,0,1:T(8,128)}, s32[11,1024]{1,0:T(8,128)}, /*index=5*/...) while((s32[]{:T(128)}, f32[4,176]{1,0:T(4,128)S(1)}, ...), condition=%wide.region_4.5_spmd.clone, body=%wide.region_1.4_spmd.clone.sunk | while | flops 379285824 | bytes 12442833 | solution.py:99
  421.3 2.0 fusion.47
  423.3 2.9 fusion.51
  426.2 1.0 fusion.49
  428.3 2.0 fusion.47
  430.2 3.0 fusion.51
  433.2 1.0 fusion.49
  435.3 2.0 fusion.47
  437.2 3.0 fusion.51
  440.2 1.0 fusion.49
  442.3 2.0 fusion.47
  444.2 3.0 fusion.51
  447.2 1.0 fusion.49
  449.3 2.0 fusion.47
  451.2 3.0 fusion.51
  454.2 1.0 fusion.49
  456.3 2.0 fusion.47
  458.2 3.0 fusion.51
  461.2 1.0 fusion.49
  463.2 2.0 fusion.47
  465.2 3.0 fusion.51
  468.2 1.0 fusion.49
  470.2 2.0 fusion.47
  472.2 3.0 fusion.51
  475.2 1.0 fusion.49
  477.2 2.0 fusion.47
  479.2 3.0 fusion.51
  482.2 1.0 fusion.49
  484.2 2.0 fusion.47
  486.2 3.0 fusion.51
  489.2 1.0 fusion.49
  491.2 2.0 fusion.47
  493.2 3.0 fusion.51
  496.2 1.0 fusion.49
  497.2 1.8 copy_bitcast_fusion
  (106 shorter events, 16.6 us)
Async XLA Ops:
  6.5 172.0 %all-gather.4.cloned.1.call-start = ((), (), s32[]{:S(2)}) async-start(), calls=%async_computation.1 | async-start | bytes 18874368 | tf_op jit(solution)/shard_map/all_gather | solution.py:41
  17.2 1.0 copy-start
  18.2 6.1 %copy-start.2 = (bf16[1024]{0:T(1024)(128)(2,1)S(1)}, bf16[1024]{0:T(1024)(128)(2,1)}, u32[]{:S(2)}) copy-start(bf16[1024]{0:T(1024)(128)(2,1)} %param.7) | copy-start | bytes 6148
  19.5 25.4 %all-to-all-start = ((bf16[4,176,1024]{2,1,0:T(8,128)(2,1)}), bf16[4,176,1024]{2,1,0:T(8,128)(2,1)S(1)}, u32[]{:S(2)}, u32[]{:S(2)}) async-start(bf16[4,176,1024]{2,1,0:T(8,128)(2,1)} %stack.2), calls=%async_computation | async-start | bytes 2883584 | tf_op jit(solution)/shard_map/all_to_all | solution.py:27
  24.3 309.9 %all-gather.6.cloned.1.call-start = ((), (), s32[]{:S(2)}) async-start(), calls=%async_computation.2 | async-start | bytes 11894784 | tf_op jit(solution)/shard_map/all_gather | solution.py:83
  185.9 11.8 %copy-start.4 = (u32[256]{0:T(256)S(1)}, u32[256]{0:T(256)}, u32[]{:S(2)}) copy-start(u32[256]{0:T(256)} %constant.56) | copy-start | bytes 3076
  185.9 12.4 %copy-start.3 = (u32[256]{0:T(256)S(1)}, u32[256]{0:T(256)}, u32[]{:S(2)}) copy-start(u32[256]{0:T(256)} %constant.61) | copy-start | bytes 3076
  185.9 14.4 %copy-start.1 = (s32[176]{0:T(256)S(1)}, s32[176]{0:T(256)}, u32[]{:S(2)}) copy-start(s32[176]{0:T(256)} %param.9) | copy-start | bytes 2116
  192.4 227.9 %all-gather.8.cloned.1.call-start = ((), (), s32[]{:S(2)}) async-start(), calls=%async_computation.3 | async-start | bytes 11894784 | tf_op jit(solution)/shard_map/all_gather | solution.py:84
Sparse Core Ops, SparseCore 0:
  17.3 161.1 all-gather.3
  192.6 115.8 all-gather.5
  311.3 109.0 all-gather.7
